TPU v7x, 512 devices: a whole 4x8x8 slice. The times are simulated.
512 devices in a mesh: chan: 8 (over z), tm: 64 (over x, y, core).
Axes of the slice: x: 4, y: 8, z: 8, core: 2. Of those that a mesh axis runs over, the one named last changes fastest.
Arguments:
- voltages: bfloat16 [8, 2, 128, 131072], P(None, None, 'chan', 'tm'), may hold values from -100 to 100
- prototype: float32 [64], replicated, may hold values from -5 to 5
- forget: float32 [8], P('chan'), may hold values from 0.5 to 16
Outputs:
- whitened: bfloat16 [8, 256, 131072], P('chan', None, 'tm')
All inputs are finite; a program needn't handle non-finite values.
Results may differ from a plain program's by a relative error of at most 0.0071.
Values may be sent and summed in bfloat16 or wider, within the bound.
No kernel may reach another device: no remote copies, remote signals or barrier semaphores. Data moves between devices by JAX's collectives and lax.ppermute only.
A program may use at most 64 MiB of HBM per device.

v0:
```python
import math

import jax
import jax.numpy as jnp
from jax import lax
from jax.sharding import PartitionSpec as P


def passed_along(value, axis, steps):
    count = lax.axis_size(axis)
    leading, last = (max(0, -steps), min(count, count - steps))
    return lax.ppermute(value, axis, [(source, source + steps) for source in range(leading, last)])


def carried_in(value, axis, join, neutral):
    count, mine = (lax.axis_size(axis), lax.axis_index(axis))
    pieces = jax.tree.map(lambda part: lax.all_gather(part, axis), value)
    total = jax.tree.map(
        lambda part, zero: jnp.full_like(part, 0) + jnp.asarray(zero, part.dtype), value, neutral
    )

    def hop(position, total):
        longer = join(total, jax.tree.map(lambda part: part[position], pieces))
        return jax.tree.map(lambda new, old: jnp.where(position < mine, new, old), longer, total)

    return lax.fori_loop(0, count - 1, hop, total)


def coefficient_table(prototype, tap_count, filter_branches):
    shaped = prototype.reshape(tap_count, filter_branches)
    steps_p = jnp.arange(filter_branches, dtype=jnp.float32)
    phase = 2.0 * math.pi / filter_branches * (steps_p[:, None] * steps_p[None, :])
    cosine = jnp.cos(phase)
    sine = jnp.sin(phase)
    pattern = jnp.stack([jnp.stack([cosine, -sine], -1), jnp.stack([sine, cosine], -1)], axis=1)
    return (shaped[:, :, None, None, None] * pattern[None]).astype(jnp.bfloat16)


def combine_stats(earlier, later):
    gram_e, count_e, retain_e = earlier
    gram_l, count_l, retain_l = later
    return (
        gram_e * retain_l[:, None, None] + gram_l,
        count_e * retain_l + count_l,
        retain_e * retain_l,
    )


def per_device(voltages, prototype, forget):
    filter_branches = voltages.shape[0]
    local_antenna_count = voltages.shape[2]
    frame_rows = voltages.shape[3]
    tap_count = prototype.shape[0] // filter_branches
    coef_table = coefficient_table(prototype, tap_count, filter_branches)
    tail_rows = passed_along(voltages[..., frame_rows - (tap_count - 1) :], "tm", 1)
    extended = jnp.concatenate([tail_rows, voltages], axis=3)
    branch_sum = jnp.zeros((filter_branches, local_antenna_count, 2, frame_rows), jnp.float32)
    for tap_idx in range(tap_count):
        branch_sum = branch_sum + jnp.einsum(
            "pcaf,pckq->kaqf",
            extended[..., tap_idx : tap_idx + frame_rows],
            coef_table[tap_idx],
            preferred_element_type=jnp.float32,
        )
    spectrum_rows = branch_sum.reshape(filter_branches, local_antenna_count * 2, frame_rows).astype(
        jnp.bfloat16
    )
    turned = lax.all_to_all(spectrum_rows, "chan", split_axis=0, concat_axis=1, tiled=True)
    channels_per_device = turned.shape[0]
    col_count = turned.shape[1]
    gram_now = jnp.einsum("cif,cjf->cij", turned, turned, preferred_element_type=jnp.float32)
    retain = jnp.exp(-forget / lax.axis_size("tm"))
    row_count = jnp.full((channels_per_device,), float(frame_rows), jnp.float32)
    zero_count = jnp.zeros((channels_per_device,), jnp.float32)
    unit_retain = jnp.ones((channels_per_device,), jnp.float32)
    prior_gram, prior_count, unused_retain = carried_in(
        (gram_now, row_count, retain),
        "tm",
        combine_stats,
        (jnp.zeros_like(gram_now), zero_count, unit_retain),
    )
    moment = retain[:, None, None] * prior_gram + gram_now
    weight_sum = retain * prior_count + jnp.float32(frame_rows)
    factor_low = jnp.linalg.cholesky(moment / weight_sum[:, None, None])
    identity_m = jnp.broadcast_to(jnp.eye(col_count, dtype=jnp.float32), factor_low.shape)
    inverse = lax.linalg.triangular_solve(factor_low, identity_m, left_side=True, lower=True)
    whitened = jnp.einsum(
        "cij,cjf->cif", inverse, turned.astype(jnp.float32), precision=lax.Precision.HIGHEST
    )
    return whitened.astype(jnp.bfloat16)


def solution(mesh):
    placed = (P(None, None, "chan", "tm"), P(), P("chan"))
    return jax.shard_map(
        per_device, mesh=mesh, in_specs=placed, out_specs=P("chan", None, "tm"), check_vma=False
    )
```

profile of v0, /device:TPU:1, one launch (start us, length us, event | category | flops | bytes accessed | tf_op | source)
XLA Modules:
  0.0 499.1 jit_solution(7681647442495996566)
XLA Ops:
  6.5 1.9 copy.32
  8.5 4.6 collective-permute-start
  14.7 2.7 collective-permute-done
  22.2 35.6 %all_to_all.4 = bf16[8,32,2048]{2,1,0:T(8,128)(2,1)S(1)} all-to-all(bf16[8,32,2048]{2,1,0:T(8,128)(2,1)S(1)} %copy.36), channel_id=1, replica_groups=mesh['chan'=8,'tm'=64] {'chan'}, dimensions={0} | all-to-all | bytes 2097152 | tf_op jit(solution)/shard_map/all_to_all | solution.py:68
  62.3 125.6 %all-reduce.3 = (f32[64]{0:T(128)S(1)}, f32[64]{0:T(128)S(1)}) all-reduce(f32[64]{0:T(128)S(1)} %fusion.66, f32[64]{0:T(128)S(1)} %dynamic-update-slice.12), channel_id=2, replica_groups=mesh['chan'=8,'tm'=64] {'tm'}, use_global_device_ids=true, to_apply=%add.1 | all-reduce | flops 128 | bytes 1024
  189.0 237.8 %while.18 = (s32[]{:T(128)}, f32[1,256,256]{2,1,0:T(8,128)S(1)}, f32[1]{0:T(128)}, s32[]{:T(128)}, f32[64,1]{0,1:T(1,128)S(1)}, /*index=5*/f32[64,1,256,256]{3,2...) while((s32[]{:T(128)}, f32[1,256,256]{2,1,0:T(8,128)S(1)}, f32[1]{0:T(128)}, s32[]{:T(128)}, ...), condition=%wide.region_1.2_spmd.clone, body=%wide.region_0.1_spmd.clone.sunk | while | flops 262151 | bytes 786610 | solution.py:26
  189.7 1.7 fusion.81
  193.5 1.7 fusion.81
  197.3 1.7 fusion.81
  201.0 1.7 fusion.81
  204.8 1.7 fusion.81
  208.6 1.7 fusion.81
  212.4 1.7 fusion.81
  216.1 1.7 fusion.81
  219.9 1.7 fusion.81
  223.7 1.7 fusion.81
  227.5 1.7 fusion.81
  235.0 1.7 fusion.81
  257.7 1.7 fusion.81
  280.3 1.7 fusion.81
  306.7 1.7 fusion.81
  329.4 1.7 fusion.81
  352.0 1.7 fusion.81
  378.4 1.7 fusion.81
  401.1 1.7 fusion.81
  423.7 1.7 fusion.81
  429.0 11.7 %custom-call.16 = f32[1,128,128]{2,1,0:T(8,128)S(1)} custom-call(f32[1,128,128]{2,1,0:T(8,128)S(1)} %cholesky.114), custom_call_target="Cholesky" | custom-call | tf_op jit(solution)/shard_map/jit(cholesky)/cholesky | solution.py:84
  440.8 9.8 %custom-call.17 = f32[1,1,128,128]{2,3,1,0:T(8,128)S(1)} custom-call(f32[1,1,128,128]{3,2,1,0:T(8,128)S(1)} %get-tuple-element.223), custom_call_target="InvertDiagBlocksLowerTriangular" | custom-call | tf_op jit(solution)/shard_map/jit(cholesky)/cholesky | solution.py:84
  451.1 11.7 %custom-call.18 = f32[1,128,128]{2,1,0:T(8,128)S(1)} custom-call(f32[1,128,128]{2,1,0:T(8,128)S(1)} %fusion.13), custom_call_target="Cholesky" | custom-call | tf_op jit(solution)/shard_map/jit(cholesky)/cholesky | solution.py:84
  465.6 4.0 while.17
  469.5 19.9 %custom-call.19 = f32[1,2,128,128]{2,3,1,0:T(8,128)S(1)} custom-call(f32[1,2,128,128]{3,2,1,0:T(8,128)S(1)} %bitcast.227), custom_call_target="InvertDiagBlocksLowerTriangular" | custom-call | tf_op jit(solution)/shard_map/triangular_solve | solution.py:86
  490.3 2.0 fusion.9
  (166 shorter events, 136.6 us)
Async XLA Ops:
  6.5 6.9 %copy-start = (bf16[8,2,16,2048]{3,2,1,0:T(8,128)(2,1)S(1)}, bf16[8,2,16,2048]{3,2,1,0:T(8,128)(2,1)}, u32[]{:S(2)}) copy-start(bf16[8,2,16,2048]{3,2,1,0:T(8,128)(2,1)} %param.5) | copy-start | bytes 3145732
  6.5 6.8 %copy-start.1 = (f32[64]{0:T(128)S(1)}, f32[64]{0:T(128)}, u32[]{:S(2)}) copy-start(f32[64]{0:T(128)} %param.6) | copy-start | bytes 772
  6.5 182.5 %all-gather.4.cloned.1.call-start = ((), (), s32[]{:S(2)}) async-start(), calls=%async_computation.1 | async-start | bytes 17039360 | tf_op jit(solution)/shard_map/all_gather | solution.py:17
  8.5 8.9 %collective-permute-start = (bf16[8,2,16,7]{3,0,1,2:T(8,128)(2,1)S(1)}, bf16[8,2,16,7]{3,0,1,2:T(8,128)(2,1)S(1)}, u32[]{:S(2)}, u32[]{:S(2)}) collective-permute-start(bf16[8,2,16,7]{3,0,1,2:T(8,128)(2,1)S(1)} %slice.121), channel_id=1, source_target_pairs={{0,1},{1,2},{2,3},{3,4},{4,5},{5,6},{6,7},{7,8},{8,9},{9,10},{10,1... | collective-permute-start | bytes 10760 | tf_op jit(solution)/shard_map/ppermute | solution.py:12
Sparse Core Ops, SparseCore 0:
  59.1 101.0 all-gather.3
where the time goes:
time: 507 us; the launch traced here: 499 us
  other arithmetic  167 us (33%)
  blocking collectives  161 us (32%)
  loops' own time  85.9 us (17%)
  local copies, waits for them, and re-layouts  52.1 us (10%)
  between operations  16.3 us (3%)
  matrix products  9.79 us (2%)
    unnamed x1, blocking collectives  126 us
    select_n x63, other arithmetic, hop(): jnp.where(position < mine, new, old)  110 us
    another operation x1, loops' own time, carried_in(): return lax.fori_loop(0, count - 1, hop, total)  85.8 us
    dynamic_slice x63, local copies, waits for them, and re-layouts, hop(): longer = join(total, jax.tree.map(lambda part: part[position], pieces))  42 us
    all_to_all x1, blocking collectives, per_device(): lax.all_to_all(spectrum_rows, 'chan', split_axis=0, concat_axis=1, tiled=...  35.6 us
    another operation x7, other arithmetic, per_device(): factor_low = jnp.linalg.cholesky(moment / weight_sum[:, None, None])  34.6 us
    another operation x3, other arithmetic, per_device(): lax.linalg.triangular_solve(factor_low, identity_m, left_side=True, lower...  19.9 us
  transfers between devices with their start and end apart: 2, of which 1 were waited for; matrix products, arithmetic and copies ran while one was open for 1% of the time, Pallas kernels for 0%

commit v1 on v0

--- a/solution.py
+++ b/solution.py
@@ -12,20 +12,6 @@
     return lax.ppermute(value, axis, [(source, source + steps) for source in range(leading, last)])
 
 
-def carried_in(value, axis, join, neutral):
-    count, mine = (lax.axis_size(axis), lax.axis_index(axis))
-    pieces = jax.tree.map(lambda part: lax.all_gather(part, axis), value)
-    total = jax.tree.map(
-        lambda part, zero: jnp.full_like(part, 0) + jnp.asarray(zero, part.dtype), value, neutral
-    )
-
-    def hop(position, total):
-        longer = join(total, jax.tree.map(lambda part: part[position], pieces))
-        return jax.tree.map(lambda new, old: jnp.where(position < mine, new, old), longer, total)
-
-    return lax.fori_loop(0, count - 1, hop, total)
-
-
 def coefficient_table(prototype, tap_count, filter_branches):
     shaped = prototype.reshape(tap_count, filter_branches)
     steps_p = jnp.arange(filter_branches, dtype=jnp.float32)
@@ -36,14 +22,17 @@
     return (shaped[:, :, None, None, None] * pattern[None]).astype(jnp.bfloat16)
 
 
-def combine_stats(earlier, later):
-    gram_e, count_e, retain_e = earlier
-    gram_l, count_l, retain_l = later
-    return (
-        gram_e * retain_l[:, None, None] + gram_l,
-        count_e * retain_l + count_l,
-        retain_e * retain_l,
-    )
+def running_mean(gram_now, forget, frame_rows):
+    count, mine = (lax.axis_size("tm"), lax.axis_index("tm"))
+    side = gram_now.shape[-1]
+    pieces = gram_now.reshape(count, side * side // (count * 128), 128)
+    every = lax.all_to_all(pieces, "tm", split_axis=0, concat_axis=0, tiled=True)
+    lag = jnp.arange(count)[:, None] - jnp.arange(count)[None, :]
+    decay = jnp.where(lag >= 0, jnp.exp(-forget[0] / count * jnp.maximum(lag, 0).astype(jnp.float32)), 0.0)
+    decay = decay / (float(frame_rows) * jnp.sum(decay, axis=1, keepdims=True))
+    mean = jnp.einsum("bc,cij->bij", decay, every, precision=lax.Precision.HIGHEST)
+    mean = lax.all_to_all(mean, "tm", split_axis=0, concat_axis=0, tiled=True)
+    return mean.reshape(gram_now.shape)
 
 
 def per_device(voltages, prototype, forget):
@@ -66,22 +55,9 @@
         jnp.bfloat16
     )
     turned = lax.all_to_all(spectrum_rows, "chan", split_axis=0, concat_axis=1, tiled=True)
-    channels_per_device = turned.shape[0]
     col_count = turned.shape[1]
     gram_now = jnp.einsum("cif,cjf->cij", turned, turned, preferred_element_type=jnp.float32)
-    retain = jnp.exp(-forget / lax.axis_size("tm"))
-    row_count = jnp.full((channels_per_device,), float(frame_rows), jnp.float32)
-    zero_count = jnp.zeros((channels_per_device,), jnp.float32)
-    unit_retain = jnp.ones((channels_per_device,), jnp.float32)
-    prior_gram, prior_count, unused_retain = carried_in(
-        (gram_now, row_count, retain),
-        "tm",
-        combine_stats,
-        (jnp.zeros_like(gram_now), zero_count, unit_retain),
-    )
-    moment = retain[:, None, None] * prior_gram + gram_now
-    weight_sum = retain * prior_count + jnp.float32(frame_rows)
-    factor_low = jnp.linalg.cholesky(moment / weight_sum[:, None, None])
+    factor_low = jnp.linalg.cholesky(running_mean(gram_now, forget, frame_rows))
     identity_m = jnp.broadcast_to(jnp.eye(col_count, dtype=jnp.float32), factor_low.shape)
     inverse = lax.linalg.triangular_solve(factor_low, identity_m, left_side=True, lower=True)
     whitened = jnp.einsum(

time: 507 us -> 158 us (0.31); the launches traced: 499 us -> 157 us
  blocking collectives: 161 us -> 35.6 us
  other arithmetic: 167 us -> 54.8 us
  loops' own time: 85.9 us -> 0.03 us
  local copies, waits for them, and re-layouts: 52.1 us -> 8.46 us
  waiting for transfers between devices: 2.72 us -> 25.8 us
  starting transfers between devices: 4.59 us -> 21.1 us
  between operations: 16.3 us -> 2.15 us
    unnamed x1 -> x0, blocking collectives: 126 us -> none
    select_n x63 -> x0, other arithmetic: 110 us -> none  [hop(): jnp.where(position < mine, new, old)]
    another operation x1 -> x0, loops' own time: 85.8 us -> none  [carried_in(): return lax.fori_loop(0, count - 1, hop, total)]
    dynamic_slice x63 -> x0, local copies, waits for them, and re-layouts: 42 us -> none  [hop(): longer = join(total, jax.tree.map(lambda part: part[position], pieces))]
    all_to_all x0 -> x2, waiting for transfers between devices: none -> 23.1 us  [the longest x1 11.9 us: running_mean(): mean = lax.all_to_all(mean, 'tm', split_axis=0, concat_axis=0, tiled=True)]
    all_to_all x0 -> x2, starting transfers between devices: none -> 16.5 us  [the longest x1 10.5 us: running_mean(): lax.all_to_all(pieces, 'tm', split_axis=0, concat_axis=0, tiled=True)]
  transfers between devices with their start and end apart: 2 -> 3, of which waited for: 1 -> 3; matrix products, arithmetic and copies ran while one was open for 1% -> 1% of each run, Pallas kernels for 0% -> 0%
where the time goes in v1:
time: 158 us; the launch traced here: 157 us
  other arithmetic  54.8 us (35%)
  blocking collectives  35.6 us (23%)
  waiting for transfers between devices  25.8 us (16%)
  starting transfers between devices  21.1 us (13%)
  matrix products  9.5 us (6%)
  local copies, waits for them, and re-layouts  8.46 us (5%)
  between operations  2.15 us (1%)
    all_to_all x1, blocking collectives, per_device(): lax.all_to_all(spectrum_rows, 'chan', split_axis=0, concat_axis=1, tiled=...  35.6 us
    another operation x7, other arithmetic, per_device(): factor_low = jnp.linalg.cholesky(running_mean(gram_now, forget, frame_rows))  34.6 us
    another operation x3, other arithmetic, per_device(): lax.linalg.triangular_solve(factor_low, identity_m, left_side=True, lower...  19.9 us
    all_to_all x1, waiting for transfers between devices, running_mean(): mean = lax.all_to_all(mean, 'tm', split_axis=0, concat_axis=0, tiled=True)  11.9 us
    all_to_all x1, waiting for transfers between devices, running_mean(): lax.all_to_all(pieces, 'tm', split_axis=0, concat_axis=0, tiled=True)  11.2 us
    all_to_all x1, starting transfers between devices, running_mean(): lax.all_to_all(pieces, 'tm', split_axis=0, concat_axis=0, tiled=True)  10.5 us
    all_to_all x1, starting transfers between devices, running_mean(): mean = lax.all_to_all(mean, 'tm', split_axis=0, concat_axis=0, tiled=True)  6.05 us
    dot_general x8, matrix products, per_device(): jnp.einsum('pcaf,pckq->kaqf', extended[..., tap_idx:tap_idx + frame_rows]...  5.35 us
  transfers between devices with their start and end apart: 3, of which 3 were waited for; matrix products, arithmetic and copies ran while one was open for 1% of the time, Pallas kernels for 0%

profile of v1, /device:TPU:1, one launch (start us, length us, event | category | flops | bytes accessed | tf_op | source)
XLA Modules:
  0.0 157.4 jit_solution(2820384755092367599)
XLA Ops:
  0.0 1.9 %copy.28 = bf16[8,2,16,2048]{3,0,1,2:T(8,128)(2,1)S(1)} copy(bf16[8,2,16,2048]{3,2,1,0:T(8,128)(2,1)} %param.3) | data formatting | bytes 2097152 | tf_op args[0]
  2.0 4.6 %collective-permute-start = (bf16[8,2,16,7]{3,0,1,2:T(8,128)(2,1)S(1)}, bf16[8,2,16,7]{3,0,1,2:T(8,128)(2,1)S(1)}, u32[]{:S(2)}, u32[]{:S(2)}) collective-permute-start(bf16[8,2,16,7]{3,0,1,2:T(8,128)(2,1)S(1)} %slice.121), channel_id=1, source_target_pairs={{0,1},{1,2},{2,3},{3,4},{4,5},{5,6},{6,7},{7,8},{8,9},{9,10},{10,1... | collective-permute-start | bytes 10760 | tf_op jit(solution)/shard_map/ppermute | solution.py:12
  6.9 1.3 convolution_bitcast_fusion
  8.2 2.7 %collective-permute-done = bf16[8,2,16,7]{3,0,1,2:T(8,128)(2,1)S(1)} collective-permute-done((bf16[8,2,16,7]{3,0,1,2:T(8,128)(2,1)S(1)}, bf16[8,2,16,7]{3,0,1,2:T(8,128)(2,1)S(1)}, u32[]{:S(2)}, u32[]{:S(2)}) %collective-permute-start) | collective-permute-done | bytes 3616 | tf_op jit(solution)/shard_map/ppermute | solution.py:12
  10.9 0.5 convolution_bitcast_fusion.1
  11.4 0.5 convolution_bitcast_fusion.2
  11.9 0.5 convolution_bitcast_fusion.3
  12.4 0.5 convolution_bitcast_fusion.4
  12.9 0.5 convolution_bitcast_fusion.5
  13.4 0.5 convolution_bitcast_fusion.6
  14.0 1.0 fusion.9
  15.1 0.6 copy.32
  15.7 35.6 %all_to_all.19 = bf16[8,32,2048]{2,1,0:T(8,128)(2,1)S(1)} all-to-all(bf16[8,32,2048]{2,1,0:T(8,128)(2,1)S(1)} %copy.32), channel_id=1, replica_groups=mesh['chan'=8,'tm'=64] {'chan'}, dimensions={0} | all-to-all | bytes 2097152 | tf_op jit(solution)/shard_map/all_to_all | solution.py:57
  51.2 0.5 fusion.79
  51.7 0.7 reshape.201
  52.4 10.5 %all-to-all-start.1 = ((f32[64,8,128]{2,1,0:T(8,128)}), f32[64,8,128]{2,1,0:T(8,128)S(1)}, u32[]{:S(2)}, u32[]{:S(2)}) async-start(f32[64,8,128]{2,1,0:T(8,128)} %reshape.201), calls=%async_computation.1 | async-start | bytes 524288 | tf_op jit(solution)/shard_map/all_to_all | solution.py:29
  63.7 11.2 %all-to-all-done.1 = f32[64,8,128]{2,1,0:T(8,128)S(1)} async-done(((f32[64,8,128]{2,1,0:T(8,128)}), f32[64,8,128]{2,1,0:T(8,128)S(1)}, u32[]{:S(2)}, u32[]{:S(2)}) %all-to-all-start.1) | async-done | bytes 262176 | tf_op jit(solution)/shard_map/all_to_all | solution.py:29
  75.3 0.9 copy.34
  76.2 6.0 %all-to-all-start.2 = ((f32[64,8,128]{2,1,0:T(8,128)}), f32[64,8,128]{2,1,0:T(8,128)S(1)}, u32[]{:S(2)}, u32[]{:S(2)}) async-start(f32[64,8,128]{2,1,0:T(8,128)} %copy.34), calls=%async_computation.2 | async-start | bytes 524288 | tf_op jit(solution)/shard_map/all_to_all | solution.py:34
  82.3 11.9 %all-to-all-done.2 = f32[64,8,128]{2,1,0:T(8,128)S(1)} async-done(((f32[64,8,128]{2,1,0:T(8,128)}), f32[64,8,128]{2,1,0:T(8,128)S(1)}, u32[]{:S(2)}, u32[]{:S(2)}) %all-to-all-start.2) | async-done | bytes 262176 | tf_op jit(solution)/shard_map/all_to_all | solution.py:34
  94.4 11.7 %custom-call.16 = f32[1,128,128]{2,1,0:T(8,128)S(1)} custom-call(f32[1,128,128]{2,1,0:T(8,128)S(1)} %cholesky.117), custom_call_target="Cholesky" | custom-call | tf_op jit(solution)/shard_map/jit(cholesky)/cholesky | solution.py:60
  106.2 9.8 %custom-call.17 = f32[1,1,128,128]{2,3,1,0:T(8,128)S(1)} custom-call(f32[1,1,128,128]{3,2,1,0:T(8,128)S(1)} %get-tuple-element.26), custom_call_target="InvertDiagBlocksLowerTriangular" | custom-call | tf_op jit(solution)/shard_map/jit(cholesky)/cholesky | solution.py:60
  116.5 11.7 %custom-call.18 = f32[1,128,128]{2,1,0:T(8,128)S(1)} custom-call(f32[1,128,128]{2,1,0:T(8,128)S(1)} %fusion.12), custom_call_target="Cholesky" | custom-call | tf_op jit(solution)/shard_map/jit(cholesky)/cholesky | solution.py:60
  128.3 0.6 compare_reduce_fusion
  128.9 0.6 compare_reduce_fusion.1
  130.8 3.8 %while.1 = (s32[]{:T(128)}, f32[1,256,256]{2,1,0:T(8,128)S(1)}, s32[2,2]{1,0:T(2,128)S(1)}, f32[2,1,128,128]{3,2,1,0:T(8,128)S(1)}, s32[]{:T(128)}) while((s32[]{:T(128)}, f32[1,256,256]{2,1,0:T(8,128)S(1)}, s32[2,2]{1,0:T(2,128)S(1)}, f32[2,1,128,128]{3,2,1,0:T(8,128)S(1)}, s32[]{:T(128)}) %tuple.24), condition=%wide.while_cond, body=%wide.while_body.sunk | while | flops 2 | bytes 131181 | solution.py:62
  130.9 0.6 fusion.88
  131.4 1.3 bitcast_dynamic-update-slice_fusion.3
  132.8 0.6 fusion.88
  133.4 1.3 bitcast_dynamic-update-slice_fusion.3
  134.7 19.9 %custom-call.19 = f32[1,2,128,128]{2,3,1,0:T(8,128)S(1)} custom-call(f32[1,2,128,128]{3,2,1,0:T(8,128)S(1)} %bitcast.198), custom_call_target="InvertDiagBlocksLowerTriangular" | custom-call | tf_op jit(solution)/shard_map/triangular_solve | solution.py:62
  155.4 2.0 %fusion.8 = bf16[1,256,2048]{2,1,0:T(8,128)(2,1)} fusion(bf16[256,2048]{1,0:T(8,128)(2,1)S(1)} %bitcast.195, f32[1,128,256]{2,1,0:T(8,128)S(1)} %convolution_bitcast_fusion.8, f32[1,128,256]{2,1,0:T(8,128)S(1)} %bitcast.197), kind=kOutput, calls=%fused_computation.25 | convolution fusion | flops 1611202560 | bytes 2359296 | tf_op jit(solution)/shard_map/cij,cjf->cif/dot_general | solution.py:63
  (35 shorter events, 2.8 us)
Async XLA Ops:
  0.0 6.9 %copy-start = (bf16[8,2,16,2048]{3,2,1,0:T(8,128)(2,1)S(1)}, bf16[8,2,16,2048]{3,2,1,0:T(8,128)(2,1)}, u32[]{:S(2)}) copy-start(bf16[8,2,16,2048]{3,2,1,0:T(8,128)(2,1)} %param.3) | copy-start | bytes 3145732
  0.0 6.8 %copy-start.1 = (f32[64]{0:T(128)S(1)}, f32[64]{0:T(128)}, u32[]{:S(2)}) copy-start(f32[64]{0:T(128)} %param.4) | copy-start | bytes 772
  2.0 8.9 %collective-permute-start = (bf16[8,2,16,7]{3,0,1,2:T(8,128)(2,1)S(1)}, bf16[8,2,16,7]{3,0,1,2:T(8,128)(2,1)S(1)}, u32[]{:S(2)}, u32[]{:S(2)}) collective-permute-start(bf16[8,2,16,7]{3,0,1,2:T(8,128)(2,1)S(1)} %slice.121), channel_id=1, source_target_pairs={{0,1},{1,2},{2,3},{3,4},{4,5},{5,6},{6,7},{7,8},{8,9},{9,10},{10,1... | collective-permute-start | bytes 10760 | tf_op jit(solution)/shard_map/ppermute | solution.py:12
  52.4 22.4 %all-to-all-start.1 = ((f32[64,8,128]{2,1,0:T(8,128)}), f32[64,8,128]{2,1,0:T(8,128)S(1)}, u32[]{:S(2)}, u32[]{:S(2)}) async-start(f32[64,8,128]{2,1,0:T(8,128)} %reshape.201), calls=%async_computation.1 | async-start | bytes 524288 | tf_op jit(solution)/shard_map/all_to_all | solution.py:29
  76.2 18.0 %all-to-all-start.2 = ((f32[64,8,128]{2,1,0:T(8,128)}), f32[64,8,128]{2,1,0:T(8,128)S(1)}, u32[]{:S(2)}, u32[]{:S(2)}) async-start(f32[64,8,128]{2,1,0:T(8,128)} %copy.34), calls=%async_computation.2 | async-start | bytes 524288 | tf_op jit(solution)/shard_map/all_to_all | solution.py:34

commit v2 on v1

v2 whole, which is shorter than its diff:
```python
import math

import jax
import jax.numpy as jnp
import numpy as np
from jax import lax
from jax.experimental import pallas as pl
from jax.experimental.pallas import tpu as pltpu
from jax.sharding import PartitionSpec as P

F32, BF16 = jnp.float32, jnp.bfloat16
LANES = 128
HALO = 128
STEP = 512
GRANT = 12 << 20
PANEL = 16


def passed_along(value, axis):
    count = lax.axis_size(axis)
    return lax.ppermute(value, axis, [(source, source + 1) for source in range(count - 1)])


def turn_pattern(branches, antennas):
    steps = np.arange(branches, dtype=np.float32)
    phase = np.float32(2.0 * math.pi / branches) * (steps[:, None] * steps[None, :])
    cosine, sine = np.cos(phase), np.sin(phase)
    pattern = np.stack([np.stack([cosine, -sine], -1), np.stack([sine, cosine], -1)], axis=1)
    wide = np.einsum("pckq,ab->kaqpcb", pattern, np.eye(antennas, dtype=np.float32))
    return wide.reshape(branches * antennas * 2, branches * 2 * antennas).astype(np.float32)


def filter_body(taps, branches, proto, pattern, tail, before, block, out, weights):
    rows, cols = pattern.shape
    step = pl.program_id(0)

    @pl.when(step == 0)
    def _():
        per_branch = cols // branches
        lane = lax.broadcasted_iota(jnp.int32, (8, cols), 1)
        for tap in range(taps):
            line = jnp.zeros((8, cols), F32)
            for branch in range(branches):
                here = (lane >= branch * per_branch) & (lane < (branch + 1) * per_branch)
                line = jnp.where(here, proto[tap * branches + branch], line)
            weights[tap] = (pattern[...] * line[:1]).astype(BF16)

    first = jnp.where(step == 0, 1, 0)
    halo = jnp.where(first == 1, tail[...], before[...])
    longer = jnp.concatenate([halo, block[...]], axis=1)
    width = block.shape[1]
    total = jnp.zeros((rows, width), F32)
    for tap in range(taps):
        start = HALO - (taps - 1) + tap
        total += jnp.dot(weights[tap], longer[:, start : start + width], preferred_element_type=F32)
    out[...] = total.astype(BF16)


def filter_bank(voltages, prototype):
    branches, parts, antennas, frames = voltages.shape
    taps = prototype.shape[0] // branches
    rows = branches * parts * antennas
    tail = passed_along(voltages[..., frames - HALO :], "tm").reshape(rows, HALO)
    flat = voltages.reshape(rows, frames)
    pattern = jnp.asarray(turn_pattern(branches, antennas))
    per = STEP // HALO
    body = lambda *refs: filter_body(taps, branches, *refs)
    return pl.pallas_call(
        body,
        out_shape=jax.ShapeDtypeStruct((rows, frames), BF16),
        grid=(frames // STEP,),
        in_specs=[
            pl.BlockSpec(memory_space=pltpu.SMEM),
            pl.BlockSpec((rows, rows), lambda i: (0, 0)),
            pl.BlockSpec((rows, HALO), lambda i: (0, 0)),
            pl.BlockSpec((rows, HALO), lambda i: (0, jnp.maximum(i * per - 1, 0))),
            pl.BlockSpec((rows, STEP), lambda i: (0, i)),
        ],
        out_specs=pl.BlockSpec((rows, STEP), lambda i: (0, i)),
        scratch_shapes=[pltpu.VMEM((taps, rows, rows), BF16)],
        compiler_params=pltpu.CompilerParams(vmem_limit_bytes=GRANT),
        name="filter_bank",
    )(prototype, pattern, tail, flat, flat)


def gram_body(x, out):
    for part in range(out.shape[0]):
        some = x[part * LANES : (part + 1) * LANES, :]
        out[part] = lax.dot_general(x[...], some, (((1,), (1,)), ((), ())), preferred_element_type=F32)


def gram(spectra):
    side = spectra.shape[0]
    return pl.pallas_call(
        gram_body,
        out_shape=jax.ShapeDtypeStruct((side // LANES, side, LANES), F32),
        in_specs=[pl.BlockSpec(memory_space=pltpu.VMEM)],
        out_specs=pl.BlockSpec(memory_space=pltpu.VMEM),
        compiler_params=pltpu.CompilerParams(vmem_limit_bytes=GRANT),
        name="gram",
    )(spectra)


def mean_body(frames, count, forget, pieces, out):
    retain = jnp.exp(jnp.full((8, LANES), -forget[0] / count, F32))
    moment = jnp.zeros((8, LANES), F32)
    weight = jnp.zeros((8, LANES), F32)
    for position in range(count):
        moment = retain * moment + pieces[position]
        weight = retain * weight + float(frames)
        out[position] = moment / weight


def running_mean(gram_now, forget, frames):
    count = lax.axis_size("tm")
    pieces = gram_now.reshape(count, -1, LANES)
    every = lax.all_to_all(pieces, "tm", split_axis=0, concat_axis=0, tiled=True)
    mean = pl.pallas_call(
        lambda *refs: mean_body(frames, count, *refs),
        out_shape=jax.ShapeDtypeStruct(every.shape, F32),
        in_specs=[pl.BlockSpec(memory_space=pltpu.SMEM), pl.BlockSpec(memory_space=pltpu.VMEM)],
        out_specs=pl.BlockSpec(memory_space=pltpu.VMEM),
        compiler_params=pltpu.CompilerParams(vmem_limit_bytes=GRANT),
        name="running_mean",
    )(forget, every)
    back = lax.all_to_all(mean, "tm", split_axis=0, concat_axis=0, tiled=True)
    return back.reshape(gram_now.shape)


def in_three(value):
    high = value.astype(BF16)
    rest = value - high.astype(F32)
    middle = rest.astype(BF16)
    return high, middle, (rest - middle.astype(F32)).astype(BF16)


def whiten_body(cov, x, y_hbm, work, inverse, y, y_sem):
    side, frames = x.shape
    half = side // 2
    work[:, :half] = cov[0]
    work[:, half:] = cov[1]
    stores = []

    def whitened(first, last):
        parts = in_three(inverse[first:last, :last])
        for at in range(0, frames, STEP):
            data = x[:last, at : at + STEP]
            total = sum(jnp.dot(part, data, preferred_element_type=F32) for part in parts)
            y[first:last, at : at + STEP] = total.astype(BF16)
            there = (slice(first, last), slice(at, at + STEP))
            store = pltpu.make_async_copy(y.at[there], y_hbm.at[there], y_sem.at[len(stores)])
            store.start()
            stores.append(store)

    lane = lax.broadcasted_iota(jnp.int32, (PANEL, side), 1)
    row = lax.broadcasted_iota(jnp.int32, (PANEL, side), 0)
    sub = lax.broadcasted_iota(jnp.int32, (PANEL, LANES), 0)
    panels = side // PANEL
    for panel in range(panels):
        at = panel * PANEL
        final = panel == panels - 1
        tall = PANEL if final else 2 * PANEL
        inside = (lane >= at) & (lane < at + PANEL)
        base = at // LANES * LANES
        near = work[at : at + tall, base : base + LANES]
        cols = [
            jnp.broadcast_to(near[:, at - base + c : at - base + c + 1], (tall, LANES))
            for c in range(PANEL)
        ]
        rows = jnp.where(inside, (lane - at == row).astype(F32), work[at : at + PANEL, :])
        if not final:
            later = jnp.where(inside, 0.0, work[at + PANEL : at + tall, :])
        scale = jnp.zeros((PANEL, LANES), F32)
        for j in range(PANEL):
            pivot = 1.0 / jnp.broadcast_to(cols[j][j : j + 1, :], (8, LANES))
            pivot = jnp.concatenate([pivot] * (tall // 8), 0)
            scale = jnp.where(sub == j, pivot[:PANEL], scale)
            if final and j == PANEL - 1:
                break
            factor = cols[j] * pivot
            for c in range(j + 1, PANEL):
                cols[c] = cols[c] - factor * jnp.broadcast_to(cols[j][c : c + 1, :], (tall, LANES))
            source = jnp.broadcast_to(rows[j : j + 1, :], (PANEL, side))
            if j < PANEL - 1:
                below = jnp.where(sub > j, factor[:PANEL], 0.0)
                rows = rows - jnp.concatenate([below] * (side // LANES), 1) * source
            if not final:
                later = later - jnp.concatenate([factor[PANEL:]] * (side // LANES), 1) * source
        scale = jnp.concatenate([scale] * (side // LANES), 1)
        inverse[at : at + PANEL, :] = jnp.where(lane < at + PANEL, rows * jnp.sqrt(scale), 0.0)
        if not final:
            work[at + PANEL : at + tall, :] = later
        if panel < panels - 2:
            rest = at + 2 * PANEL
            cut = rest // LANES * LANES
            a, b, c = in_three((rows * scale)[:, cut:])
            d, e, f = in_three(rows)
            update = lax.dot_general(
                jnp.concatenate([a, a, b, b, a, c], 0),
                jnp.concatenate([d, e, d, e, f, d], 0),
                (((0,), (0,)), ((), ())),
                preferred_element_type=F32,
            )
            wide = lax.broadcasted_iota(jnp.int32, (side - rest, side), 1)
            held = jnp.where((wide >= at) & (wide < at + PANEL), 0.0, work[rest:, :])
            work[rest:, :] = held - update[rest - cut :]
        if panel == panels // 2 - 1:
            whitened(0, half)
    whitened(half, side)
    for store in stores:
        store.wait()


def whiten(cov, spectra):
    side, frames = spectra.shape
    chunks = 2 * (frames // STEP)
    return pl.pallas_call(
        whiten_body,
        out_shape=jax.ShapeDtypeStruct(spectra.shape, BF16),
        in_specs=[pl.BlockSpec(memory_space=pltpu.VMEM)] * 2,
        out_specs=pl.BlockSpec(memory_space=pl.ANY),
        scratch_shapes=[
            pltpu.VMEM((side, side), F32),
            pltpu.VMEM((side, side), F32),
            pltpu.VMEM((side, frames), BF16),
            pltpu.SemaphoreType.DMA((chunks,)),
        ],
        compiler_params=pltpu.CompilerParams(vmem_limit_bytes=GRANT),
        name="whiten",
    )(cov, spectra)


def per_device(voltages, prototype, forget):
    frames = voltages.shape[3]
    channels = lax.axis_size("chan")
    spectra = filter_bank(voltages, prototype).reshape(channels, -1, frames)
    turned = lax.all_to_all(spectra, "chan", split_axis=0, concat_axis=0, tiled=True)
    turned = turned.reshape(-1, frames)
    mean = running_mean(gram(turned), forget, frames)
    return whiten(mean, turned)[None]


def solution(mesh):
    placed = (P(None, None, "chan", "tm"), P(), P("chan"))
    return jax.shard_map(
        per_device, mesh=mesh, in_specs=placed, out_specs=P("chan", None, "tm"), check_vma=False
    )
```

time: 158 us -> 102 us (0.65)
  other arithmetic: 54.8 us -> 0 us
  blocking collectives: 35.6 us -> 52.6 us
  Pallas kernels: 0 us -> 13.6 us
  waiting for transfers between devices: 25.8 us -> 15.6 us
  matrix products: 9.5 us -> 0 us
  starting transfers between devices: 21.1 us -> 15.5 us
  local copies, waits for them, and re-layouts: 8.46 us -> 3.67 us
    another operation x12 -> x0, other arithmetic: 54.5 us -> none  [the longest x7 34.6 us: per_device(): factor_low = jnp.linalg.cholesky(running_mean(gram_now, forget, frame_rows))]
    all_to_all x1 -> x2, blocking collectives: 35.6 us -> 52.6 us  [the longest x1 34.8 us: per_device(): lax.all_to_all(spectra, 'chan', split_axis=0, concat_axis=0, tiled=True)]
    pallas_call x0 -> x4, Pallas kernels: none -> 13.6 us  [the longest x1 6.87 us: whiten(): pl.pallas_call(whiten_body, out_shape=jax.ShapeDtypeStruct(spectra.shape,...]
    all_to_all x1 -> x0, waiting for transfers between devices: 11.9 us -> none  [running_mean(): mean = lax.all_to_all(mean, 'tm', split_axis=0, concat_axis=0, tiled=True)]
    dot_general x11 -> x0, matrix products: 8.19 us -> none  [the longest x8 5.35 us: per_device(): jnp.einsum('pcaf,pckq->kaqf', extended[..., tap_idx:tap_idx + frame_rows]...]
    all_to_all x1 -> x0, starting transfers between devices: 6.05 us -> none  [running_mean(): mean = lax.all_to_all(mean, 'tm', split_axis=0, concat_axis=0, tiled=True)]
    another operation x10 -> x0, local copies, waits for them, and re-layouts: 3.95 us -> none
    ppermute x1, waiting for transfers between devices: 2.69 us -> 4.27 us  [passed_along(): lax.ppermute(value, axis, [(source, source + 1) for source in range(count...]
  transfers between devices with their start and end apart: 3 -> 2, of which waited for: 3 -> 2; matrix products, arithmetic and copies ran while one was open for 1% -> 0% of each run, Pallas kernels for 0% -> 0%
where the time goes in v2:
time: 102 us
  blocking collectives  52.6 us (52%)
  waiting for transfers between devices  15.6 us (15%)
  starting transfers between devices  15.5 us (15%)
  Pallas kernels  13.6 us (13%)
  local copies, waits for them, and re-layouts  3.67 us (4%)
    all_to_all x1, blocking collectives, per_device(): lax.all_to_all(spectra, 'chan', split_axis=0, concat_axis=0, tiled=True)  34.8 us
    all_to_all x1, blocking collectives, running_mean(): back = lax.all_to_all(mean, 'tm', split_axis=0, concat_axis=0, tiled=True)  17.8 us
    all_to_all x1, waiting for transfers between devices, running_mean(): lax.all_to_all(pieces, 'tm', split_axis=0, concat_axis=0, tiled=True)  11.3 us
    all_to_all x1, starting transfers between devices, running_mean(): lax.all_to_all(pieces, 'tm', split_axis=0, concat_axis=0, tiled=True)  10.9 us
    pallas_call x1, Pallas kernels, whiten(): pl.pallas_call(whiten_body, out_shape=jax.ShapeDtypeStruct(spectra.shape,...  6.87 us
    pallas_call x1, Pallas kernels, filter_bank(): pl.pallas_call(body, out_shape=jax.ShapeDtypeStruct((rows, frames), BF16)...  5.23 us
    ppermute x1, starting transfers between devices, passed_along(): lax.ppermute(value, axis, [(source, source + 1) for source in range(count...  4.57 us
    ppermute x1, waiting for transfers between devices, passed_along(): lax.ppermute(value, axis, [(source, source + 1) for source in range(count...  4.27 us
  transfers between devices with their start and end apart: 2, of which 2 were waited for; matrix products, arithmetic and copies ran while one was open for 0% of the time, Pallas kernels for 0%

profile of v2, /device:TPU:1, one launch (start us, length us, event | category | flops | bytes accessed | tf_op | source)
XLA Modules:
  0.0 101.7 jit_solution(17354405137788088786)
XLA Ops:
  0.0 0.8 slice.3
  0.8 4.6 %collective-permute-start = (bf16[8,2,16,128]{3,2,1,0:T(8,128)(2,1)S(1)}, bf16[8,2,16,128]{3,2,1,0:T(8,128)(2,1)S(1)}, u32[]{:S(2)}, u32[]{:S(2)}) collective-permute-start(bf16[8,2,16,128]{3,2,1,0:T(8,128)(2,1)S(1)} %slice.3), channel_id=1, source_target_pairs={{0,1},{1,2},{2,3},{3,4},{4,5},{5,6},{6,7},{7,8},{8,9},{9,10},{10,1... | collective-permute-start | bytes 196616 | tf_op jit(solution)/shard_map/ppermute | solution.py:21
  5.4 4.3 %collective-permute-done = bf16[8,2,16,128]{3,2,1,0:T(8,128)(2,1)S(1)} collective-permute-done((bf16[8,2,16,128]{3,2,1,0:T(8,128)(2,1)S(1)}, bf16[8,2,16,128]{3,2,1,0:T(8,128)(2,1)S(1)}, u32[]{:S(2)}, u32[]{:S(2)}) %collective-permute-start) | collective-permute-done | bytes 65568 | tf_op jit(solution)/shard_map/ppermute | solution.py:21
  9.7 0.0 copy-start.2
  9.7 0.7 copy-done.2
  10.4 0.0 copy-start
  10.4 1.2 %copy-done = bf16[8,2,16,2048]{3,2,1,0:T(8,128)(2,1)S(1)} copy-done((bf16[8,2,16,2048]{3,2,1,0:T(8,128)(2,1)S(1)}, bf16[8,2,16,2048]{3,2,1,0:T(8,128)(2,1)}, u32[]{:S(2)}) %copy-start) | copy-done | bytes 1048600
  11.6 0.0 copy-start.1
  11.6 0.9 copy-done.1
  12.5 5.2 %filter_bank.1 = bf16[256,2048]{1,0:T(8,128)(2,1)S(1)} custom-call(f32[64]{0:T(128)S(1)} %copy-done.2, f32[256,256]{1,0:T(8,128)S(1)} %copy-done.1, bf16[256,128]{1,0:T(8,128)(2,1)S(1)} %bitcast.13, bf16[256,2048]{1,0:T(8,128)(2,1)S(1)} %bitcast.9, bf16[256,2048]{1,0:T(8,128)(2,1)S(1)} %bitcast.10), custom_call_target="tpu_custom_call" | custom-call | tf_op jit(solution)/shard_map/filter_bank/pallas_call | solution.py:68
  17.8 34.8 %all_to_all.15 = bf16[8,32,2048]{2,1,0:T(8,128)(2,1)S(1)} all-to-all(bf16[8,32,2048]{2,1,0:T(8,128)(2,1)S(1)} %bitcast.11), channel_id=1, replica_groups=mesh['chan'=8,'tm'=64] {'chan'}, dimensions={0} | all-to-all | bytes 2097152 | tf_op jit(solution)/shard_map/all_to_all | solution.py:237
  52.6 1.4 %gram.1 = f32[2,256,128]{2,1,0:T(8,128)} custom-call(bf16[256,2048]{1,0:T(8,128)(2,1)S(1)} %bitcast.7), custom_call_target="tpu_custom_call" | custom-call | tf_op jit(solution)/shard_map/gram/pallas_call | solution.py:94
  54.0 10.9 %all-to-all-start.1 = ((f32[64,8,128]{2,1,0:T(8,128)}), f32[64,8,128]{2,1,0:T(8,128)S(1)}, u32[]{:S(2)}, u32[]{:S(2)}) async-start(f32[64,8,128]{2,1,0:T(8,128)} %bitcast.4), calls=%async_computation.1 | async-start | bytes 524288 | tf_op jit(solution)/shard_map/all_to_all | solution.py:117
  65.6 11.3 %all-to-all-done.1.refs_1_ = f32[64,8,128]{2,1,0:T(8,128)S(1)} async-done(((f32[64,8,128]{2,1,0:T(8,128)}), f32[64,8,128]{2,1,0:T(8,128)S(1)}, u32[]{:S(2)}, u32[]{:S(2)}) %all-to-all-start.1) | async-done | bytes 262176 | tf_op jit(solution)/shard_map/all_to_all | solution.py:117
  76.9 0.1 running_mean.1
  77.1 17.8 %all_to_all.16 = f32[64,8,128]{2,1,0:T(8,128)S(1)} all-to-all(f32[64,8,128]{2,1,0:T(8,128)S(1)} %running_mean.1), channel_id=1, replica_groups=mesh['chan'=8,'tm'=64] {'tm'}, dimensions={0} | all-to-all | bytes 524288 | tf_op jit(solution)/shard_map/all_to_all | solution.py:126
  94.9 6.9 %whiten.1 = bf16[256,2048]{1,0:T(8,128)(2,1)} custom-call(f32[2,256,128]{2,1,0:T(8,128)S(1)} %bitcast.12, bf16[256,2048]{1,0:T(8,128)(2,1)S(1)} %bitcast.8), custom_call_target="tpu_custom_call" | custom-call | tf_op jit(solution)/shard_map/whiten/pallas_call | solution.py:217
Async XLA Ops:
  0.8 8.9 %collective-permute-start = (bf16[8,2,16,128]{3,2,1,0:T(8,128)(2,1)S(1)}, bf16[8,2,16,128]{3,2,1,0:T(8,128)(2,1)S(1)}, u32[]{:S(2)}, u32[]{:S(2)}) collective-permute-start(bf16[8,2,16,128]{3,2,1,0:T(8,128)(2,1)S(1)} %slice.3), channel_id=1, source_target_pairs={{0,1},{1,2},{2,3},{3,4},{4,5},{5,6},{6,7},{7,8},{8,9},{9,10},{10,1... | collective-permute-start | bytes 196616 | tf_op jit(solution)/shard_map/ppermute | solution.py:21
  9.7 0.7 copy-start.2
  10.4 1.2 %copy-start = (bf16[8,2,16,2048]{3,2,1,0:T(8,128)(2,1)S(1)}, bf16[8,2,16,2048]{3,2,1,0:T(8,128)(2,1)}, u32[]{:S(2)}) copy-start(bf16[8,2,16,2048]{3,2,1,0:T(8,128)(2,1)} %param.4) | copy-start | bytes 3145732
  11.6 0.9 copy-start.1
  54.0 22.9 %all-to-all-start.1 = ((f32[64,8,128]{2,1,0:T(8,128)}), f32[64,8,128]{2,1,0:T(8,128)S(1)}, u32[]{:S(2)}, u32[]{:S(2)}) async-start(f32[64,8,128]{2,1,0:T(8,128)} %bitcast.4), calls=%async_computation.1 | async-start | bytes 524288 | tf_op jit(solution)/shard_map/all_to_all | solution.py:117

commit v3 on v2

v3 whole, which is shorter than its diff:
```python
import math

import jax
import jax.numpy as jnp
import numpy as np
from jax import lax
from jax.experimental import pallas as pl
from jax.experimental.pallas import tpu as pltpu
from jax.sharding import PartitionSpec as P

F32, BF16 = jnp.float32, jnp.bfloat16
LANES = 128
LOWEST = float(np.finfo(np.float32).min)
HALO = 128
STEP = 512
GRANT = 12 << 20
PANEL = 16


def passed_along(value, axis):
    count = lax.axis_size(axis)
    return lax.ppermute(value, axis, [(source, source + 1) for source in range(count - 1)])


def turn_pattern(branches, antennas):
    steps = np.arange(branches, dtype=np.float32)
    phase = np.float32(2.0 * math.pi / branches) * (steps[:, None] * steps[None, :])
    cosine, sine = np.cos(phase), np.sin(phase)
    pattern = np.stack([np.stack([cosine, -sine], -1), np.stack([sine, cosine], -1)], axis=1)
    lines = pattern.transpose(2, 3, 0, 1).reshape(branches * 2, branches * 2)
    return np.repeat(lines, antennas, axis=1).astype(np.float32)


def tap_weights(proto, pattern, weights, branches, antennas):
    cols = pattern.shape[1]
    taps = weights.shape[1] // cols
    per_branch = cols // branches
    lane = lax.broadcasted_iota(jnp.int32, (8, cols), 1)
    lines = []
    for tap in range(taps):
        line = jnp.zeros((8, cols), F32)
        for branch in range(branches):
            here = (lane >= branch * per_branch) & (lane < (branch + 1) * per_branch)
            line = jnp.where(here, proto[tap * branches + branch], line)
        lines.append(jnp.broadcast_to(line[:1], (2 * antennas, cols)))
    shape = (2 * antennas, cols)
    part = lax.broadcasted_iota(jnp.int32, shape, 0) & 1
    antenna = lax.broadcasted_iota(jnp.int32, shape, 0) >> 1
    same = antenna == (lax.broadcasted_iota(jnp.int32, shape, 1) & (antennas - 1))
    for channel in range(branches):
        real = jnp.broadcast_to(pattern[2 * channel : 2 * channel + 1, :], shape)
        imag = jnp.broadcast_to(pattern[2 * channel + 1 : 2 * channel + 2, :], shape)
        turn = jnp.where(same, jnp.where(part == 0, real, imag), 0.0)
        rows = slice(channel * 2 * antennas, (channel + 1) * 2 * antennas)
        for tap in range(taps):
            weights[rows, tap * cols : (tap + 1) * cols] = (turn * lines[tap]).astype(BF16)


def filtered(weights, longer, width):
    rows = longer.shape[0]
    taps = weights.shape[1] // rows
    first = longer.shape[1] - width - (taps - 1)
    total = jnp.zeros((weights.shape[0], width), F32)
    for tap in range(taps):
        data = longer[:, first + tap : first + tap + width]
        total += jnp.dot(weights[:, tap * rows : (tap + 1) * rows], data, preferred_element_type=F32)
    return total.astype(BF16)


def filter_body(branches, antennas, count, proto, forget, pattern, x_hbm, out, weights, start, retain, x, sems):
    rows, frames = x_hbm.shape
    fetches = []
    for at in range(0, frames, STEP):
        there = (slice(None), slice(at, at + STEP))
        fetches.append(pltpu.make_async_copy(x_hbm.at[there], x.at[there], sems.at[at // STEP]))
        fetches[-1].start()
    tap_weights(proto, pattern, weights, branches, antennas)
    for at in range(0, frames, STEP):
        fetches[at // STEP].wait()
        halo = x[:, at - HALO : at] if at else jnp.zeros((rows, HALO), BF16)
        longer = jnp.concatenate([halo, x[:, at : at + STEP]], axis=1)
        out[:, at : at + STEP] = filtered(weights, longer, STEP)
    start[...] = x[:, :HALO]
    retain[...] = jnp.exp(jnp.full(retain.shape, -forget[0] / count, F32))


def filter_bank(flat, prototype, forget, branches, antennas):
    rows, frames = flat.shape
    taps = prototype.shape[0] // branches
    pattern = jnp.asarray(turn_pattern(branches, antennas))
    count = lax.axis_size("tm")
    smem = pl.BlockSpec(memory_space=pltpu.SMEM)
    vmem = pl.BlockSpec(memory_space=pltpu.VMEM)
    return pl.pallas_call(
        lambda *refs: filter_body(branches, antennas, count, *refs),
        out_shape=(
            jax.ShapeDtypeStruct((rows, frames), BF16),
            jax.ShapeDtypeStruct((rows, rows * taps), BF16),
            jax.ShapeDtypeStruct((rows, HALO), BF16),
            jax.ShapeDtypeStruct((8, LANES), F32),
        ),
        in_specs=[smem, smem, vmem, pl.BlockSpec(memory_space=pltpu.HBM)],
        out_specs=(vmem,) * 4,
        scratch_shapes=[
            pltpu.VMEM((rows, frames), BF16),
            pltpu.SemaphoreType.DMA((frames // STEP,)),
        ],
        compiler_params=pltpu.CompilerParams(vmem_limit_bytes=GRANT),
        cost_estimate=pl.CostEstimate(
            flops=2 * taps * rows * rows * frames, bytes_accessed=4 * rows * frames, transcendentals=0
        ),
        name="filter_bank",
    )(prototype, forget, pattern, pltpu.with_memory_space_constraint(flat, pltpu.HBM))


def head_body(tail, start, weights, alone, out):
    longer = jnp.concatenate([tail[...], start[...]], axis=1)
    out[...] = filtered(weights, longer, HALO)


def with_history(alone, weights, start, tail):
    rows, frames = alone.shape
    vmem = pl.BlockSpec(memory_space=pltpu.VMEM)
    head = pl.BlockSpec((rows, HALO), lambda i: (0, 0))
    return pl.pallas_call(
        head_body,
        out_shape=jax.ShapeDtypeStruct((rows, frames), BF16),
        grid=(1,),
        in_specs=[vmem, vmem, vmem, pl.BlockSpec(memory_space=pl.ANY)],
        out_specs=head,
        input_output_aliases={3: 0},
        compiler_params=pltpu.CompilerParams(vmem_limit_bytes=GRANT),
        name="with_history",
    )(tail, start, weights, alone)


def gram_body(x, out):
    for part in range(out.shape[0]):
        some = x[part * LANES : (part + 1) * LANES, :]
        out[part] = lax.dot_general(x[...], some, (((1,), (1,)), ((), ())), preferred_element_type=F32)


def gram(spectra):
    side = spectra.shape[0]
    vmem = pl.BlockSpec(memory_space=pltpu.VMEM)
    return pl.pallas_call(
        gram_body,
        out_shape=jax.ShapeDtypeStruct((side // LANES, side, LANES), F32),
        in_specs=[vmem],
        out_specs=vmem,
        compiler_params=pltpu.CompilerParams(vmem_limit_bytes=GRANT),
        name="gram",
    )(spectra)


def mean_body(frames, retained, pieces, out):
    retain = retained[...]
    moment = jnp.zeros((8, LANES), F32)
    weight = jnp.zeros((8, LANES), F32)
    for position in range(pieces.shape[0]):
        moment = retain * moment + pieces[position]
        weight = retain * weight + float(frames)
        out[position] = moment / weight


def running_mean(gram_now, retained, frames):
    count = lax.axis_size("tm")
    pieces = gram_now.reshape(count, -1, LANES)
    every = lax.all_to_all(pieces, "tm", split_axis=0, concat_axis=0, tiled=True)
    mean = pl.pallas_call(
        lambda *refs: mean_body(frames, *refs),
        out_shape=jax.ShapeDtypeStruct(every.shape, F32),
        in_specs=[pl.BlockSpec(memory_space=pltpu.VMEM)] * 2,
        out_specs=pl.BlockSpec(memory_space=pltpu.VMEM),
        compiler_params=pltpu.CompilerParams(vmem_limit_bytes=GRANT),
        name="running_mean",
    )(retained, every)
    back = lax.all_to_all(mean, "tm", split_axis=0, concat_axis=0, tiled=True)
    return back.reshape(gram_now.shape)


def in_three(value):
    high = value.astype(BF16)
    rest = value - high.astype(F32)
    middle = rest.astype(BF16)
    return high, middle, (rest - middle.astype(F32)).astype(BF16)


def whiten_body(cov, x, y_hbm, work, inverse, y, y_sem):
    side, frames = x.shape
    half = side // 2
    work[:, :half] = cov[0]
    work[:, half:] = cov[1]
    stores = []

    def whitened(first, last):
        parts = in_three(inverse[first:last, :last])
        for at in range(0, frames, STEP):
            data = x[:last, at : at + STEP]
            total = sum(jnp.dot(part, data, preferred_element_type=F32) for part in parts)
            y[first:last, at : at + STEP] = total.astype(BF16)
            there = (slice(first, last), slice(at, at + STEP))
            store = pltpu.make_async_copy(y.at[there], y_hbm.at[there], y_sem.at[len(stores)])
            store.start()
            stores.append(store)

    lane = lax.broadcasted_iota(jnp.int32, (PANEL, side), 1)
    row = lax.broadcasted_iota(jnp.int32, (PANEL, side), 0)
    sub = lax.broadcasted_iota(jnp.int32, (8, LANES), 0)
    panels = side // PANEL
    own = PANEL // 8

    def eights(value):
        return [value[r : r + 8] for r in range(0, value.shape[0], 8)]

    def line(tile, at):
        return jnp.broadcast_to(tile[at : at + 1, :], tile.shape)

    def across(tile):
        return jnp.concatenate([tile] * (side // LANES), 1)

    for panel in range(panels):
        at = panel * PANEL
        final = panel == panels - 1
        tall = PANEL if final else 2 * PANEL
        inside = (lane >= at) & (lane < at + PANEL)
        base = at // LANES * LANES
        near = work[at : at + tall, base : base + LANES]
        cols = []
        for c in range(PANEL):
            spread = jnp.broadcast_to(near[:, at - base + c : at - base + c + 1], (tall, LANES))
            cols.append(eights(jnp.maximum(spread, LOWEST)))
        rows = eights(jnp.where(inside, (lane - at == row).astype(F32), work[at : at + PANEL, :]))
        later = []
        if not final:
            later = eights(jnp.where(inside, 0.0, work[at + PANEL : at + tall, :]))
        scale = [jnp.zeros((8, LANES), F32)] * own
        for j in range(PANEL):
            top = j // 8
            pivot = 1.0 / line(cols[j][top], j % 8)
            scale[top] = jnp.where(sub == j % 8, pivot, scale[top])
            factor = [None if r < top else tile * pivot for r, tile in enumerate(cols[j])]
            for c in range(j + 1, PANEL):
                shared = line(cols[j][c // 8], c % 8)
                for r in range(c // 8, tall // 8):
                    cols[c][r] = cols[c][r] - factor[r] * shared
            source = line(rows[top], j % 8)
            for r in range(top, own):
                below = jnp.where(sub > j % 8, factor[r], 0.0) if r == top else factor[r]
                rows[r] = rows[r] - across(below) * source
            for r in range(len(later)):
                later[r] = later[r] - across(factor[own + r]) * source
        rows = jnp.concatenate(rows, 0)
        scale = jnp.concatenate(scale, 0)
        scale = jnp.concatenate([scale] * (side // LANES), 1)
        inverse[at : at + PANEL, :] = jnp.where(lane < at + PANEL, rows * jnp.sqrt(scale), 0.0)
        if not final:
            work[at + PANEL : at + tall, :] = jnp.concatenate(later, 0)
        if panel < panels - 2:
            rest = at + 2 * PANEL
            cut = rest // LANES * LANES
            a, b, c = in_three((rows * scale)[:, cut:])
            d, e, f = in_three(rows)
            update = lax.dot_general(
                jnp.concatenate([a, a, b, b, a, c], 0),
                jnp.concatenate([d, e, d, e, f, d], 0),
                (((0,), (0,)), ((), ())),
                preferred_element_type=F32,
            )
            wide = lax.broadcasted_iota(jnp.int32, (side - rest, side), 1)
            held = jnp.where((wide >= at) & (wide < at + PANEL), 0.0, work[rest:, :])
            work[rest:, :] = held - update[rest - cut :]
        if (panel + 1) % (panels // 4) == 0 and panel > panels // 4:
            done = at + PANEL
            whitened(0 if done == half else done - side // 4, done)
    for store in stores:
        store.wait()


def whiten(cov, spectra):
    side, frames = spectra.shape
    chunks = 3 * (frames // STEP)
    return pl.pallas_call(
        whiten_body,
        out_shape=jax.ShapeDtypeStruct(spectra.shape, BF16),
        in_specs=[pl.BlockSpec(memory_space=pltpu.VMEM)] * 2,
        out_specs=pl.BlockSpec(memory_space=pl.ANY),
        scratch_shapes=[
            pltpu.VMEM((side, side), F32),
            pltpu.VMEM((side, side), F32),
            pltpu.VMEM((side, frames), BF16),
            pltpu.SemaphoreType.DMA((chunks,)),
        ],
        compiler_params=pltpu.CompilerParams(vmem_limit_bytes=GRANT),
        name="whiten",
    )(cov, spectra)


def per_device(voltages, prototype, forget):
    branches, parts, antennas, frames = voltages.shape
    flat = voltages.reshape(-1, frames)
    tail = passed_along(flat[:, frames - HALO :], "tm")
    alone, weights, start, retained = filter_bank(flat, prototype, forget, branches, antennas)
    spectra = with_history(alone, weights, start, tail).reshape(branches, -1, frames)
    turned = lax.all_to_all(spectra, "chan", split_axis=0, concat_axis=0, tiled=True)
    turned = turned.reshape(-1, frames)
    mean = running_mean(gram(turned), retained, frames)
    return whiten(mean, turned)[None]


def solution(mesh):
    placed = (P(None, None, "chan", "tm"), P(), P("chan"))
    return jax.shard_map(
        per_device, mesh=mesh, in_specs=placed, out_specs=P("chan", None, "tm"), check_vma=False
    )
```

time: 102 us -> 98.5 us (0.966)
  blocking collectives: 52.6 us -> 78.3 us
  waiting for transfers between devices: 15.6 us -> 0.01 us
  starting transfers between devices: 15.5 us -> 4.7 us
  local copies, waits for them, and re-layouts: 3.67 us -> 0.86 us
    all_to_all x0 -> x1, blocking collectives: none -> 22.3 us  [running_mean(): lax.all_to_all(pieces, 'tm', split_axis=0, concat_axis=0, tiled=True)]
    all_to_all x1 -> x0, waiting for transfers between devices: 11.3 us -> none  [running_mean(): lax.all_to_all(pieces, 'tm', split_axis=0, concat_axis=0, tiled=True)]
    all_to_all x1 -> x0, starting transfers between devices: 10.9 us -> none  [running_mean(): lax.all_to_all(pieces, 'tm', split_axis=0, concat_axis=0, tiled=True)]
    ppermute x1, waiting for transfers between devices: 4.27 us -> 0.01 us  [passed_along(): lax.ppermute(value, axis, [(source, source + 1) for source in range(count...]
    all_to_all x1, blocking collectives: 34.8 us -> 38.2 us  [per_device(): lax.all_to_all(spectra, 'chan', split_axis=0, concat_axis=0, tiled=True)]
    unnamed x6 -> x4, local copies, waits for them, and re-layouts: 2.83 us -> 0.01 us
    pallas_call x2 -> x3, Pallas kernels: 5.37 us -> 6.3 us  [the longest x1 5.59 us: filter_bank(): pl.pallas_call(lambda *refs: filter_body(branches, antennas, count, *refs...]
  transfers between devices with their start and end apart: 2 -> 1, of which waited for: 2 -> 0; matrix products, arithmetic and copies ran while one was open for 0% -> 0% of each run, Pallas kernels for 0% -> 6%
where the time goes in v3:
time: 98.5 us; the launch traced here: 98.2 us
  blocking collectives  78.3 us (79%)
  Pallas kernels  13.6 us (14%)
  starting transfers between devices  4.7 us (5%)
    all_to_all x1, blocking collectives, per_device(): lax.all_to_all(spectra, 'chan', split_axis=0, concat_axis=0, tiled=True)  38.2 us
    all_to_all x1, blocking collectives, running_mean(): lax.all_to_all(pieces, 'tm', split_axis=0, concat_axis=0, tiled=True)  22.3 us
    all_to_all x1, blocking collectives, running_mean(): back = lax.all_to_all(mean, 'tm', split_axis=0, concat_axis=0, tiled=True)  17.8 us
    pallas_call x1, Pallas kernels, whiten(): pl.pallas_call(whiten_body, out_shape=jax.ShapeDtypeStruct(spectra.shape,...  6.6 us
    pallas_call x1, Pallas kernels, filter_bank(): pl.pallas_call(lambda *refs: filter_body(branches, antennas, count, *refs...  5.59 us
    ppermute x1, starting transfers between devices, passed_along(): lax.ppermute(value, axis, [(source, source + 1) for source in range(count...  4.7 us
  transfers between devices with their start and end apart: 1, of which 0 were waited for; matrix products, arithmetic and copies ran while one was open for 0% of the time, Pallas kernels for 6%

profile of v3, /device:TPU:1, one launch (start us, length us, event | category | flops | bytes accessed | tf_op | source)
XLA Modules:
  0.0 98.2 jit_solution(7037111434290571069)
XLA Ops:
  0.0 0.0 copy-start.1
  0.0 0.9 slice.4
  0.9 0.0 copy-start
  0.9 4.7 %collective-permute-start = (bf16[256,128]{1,0:T(8,128)(2,1)S(1)}, bf16[256,128]{1,0:T(8,128)(2,1)S(1)}, u32[]{:S(2)}, u32[]{:S(2)}) collective-permute-start(bf16[256,128]{1,0:T(8,128)(2,1)S(1)} %slice.4), channel_id=1, source_target_pairs={{0,1},{1,2},{2,3},{3,4},{4,5},{5,6},{6,7},{7,8},{8,9},{9,10},{10,1... | collective-permute-start | bytes 196616 | tf_op jit(solution)/shard_map/ppermute | solution.py:22
  6.2 0.0 copy-done.1
  6.2 0.0 copy-done
  6.2 5.6 %filter_bank.1 = (bf16[256,2048]{1,0:T(8,128)(2,1)S(1)}, bf16[256,2048]{1,0:T(8,128)(2,1)S(1)}, bf16[256,128]{1,0:T(8,128)(2,1)S(1)}, f32[8,128]{1,0:T(8,128)S(1)}) custom-call(f32[64]{0:T(128)S(1)} %copy-done, f32[1]{0:T(128)S(6)} %copy.7.refs_1_, f32[16,256]{1,0:T(8,128)S(1)} %copy-done.1, bf16[256,2048]{1,0:T(8,128)(2,1)} %bitcast.12), custom_call_target="tpu_custom_call" | custom-call | flops 2147483648 | bytes 2097152 | tf_op jit(solution)/shard_map/filter_bank/pallas_call | solution.py:94
  11.8 0.0 collective-permute-done.tail
  11.8 0.6 with_history.1
  12.4 38.2 %all_to_all.15 = bf16[8,32,2048]{2,1,0:T(8,128)(2,1)S(1)} all-to-all(bf16[8,32,2048]{2,1,0:T(8,128)(2,1)S(1)} %bitcast.8), channel_id=1, replica_groups=mesh['chan'=8,'tm'=64] {'chan'}, dimensions={0} | all-to-all | bytes 2097152 | tf_op jit(solution)/shard_map/all_to_all | solution.py:305
  50.7 0.7 gram.1
  51.4 22.3 %all_to_all.16.refs_1_ = f32[64,8,128]{2,1,0:T(8,128)S(1)} all-to-all(f32[64,8,128]{2,1,0:T(8,128)S(1)} %bitcast.10), channel_id=1, replica_groups=mesh['chan'=8,'tm'=64] {'tm'}, dimensions={0} | all-to-all | bytes 524288 | tf_op jit(solution)/shard_map/all_to_all | solution.py:169
  73.6 0.1 running_mean.1
  73.8 17.8 %all_to_all.17 = f32[64,8,128]{2,1,0:T(8,128)S(1)} all-to-all(f32[64,8,128]{2,1,0:T(8,128)S(1)} %running_mean.1), channel_id=1, replica_groups=mesh['chan'=8,'tm'=64] {'tm'}, dimensions={0} | all-to-all | bytes 524288 | tf_op jit(solution)/shard_map/all_to_all | solution.py:178
  91.6 6.6 %whiten.1 = bf16[256,2048]{1,0:T(8,128)(2,1)} custom-call(f32[2,256,128]{2,1,0:T(8,128)S(1)} %bitcast.9, bf16[256,2048]{1,0:T(8,128)(2,1)S(1)} %bitcast.7), custom_call_target="tpu_custom_call" | custom-call | tf_op jit(solution)/shard_map/whiten/pallas_call | solution.py:283
Async XLA Ops:
  0.0 6.2 %copy-start.1 = (f32[16,256]{1,0:T(8,128)S(1)}, f32[16,256]{1,0:T(8,128)}, u32[]{:S(2)}) copy-start(f32[16,256]{1,0:T(8,128)} %constant.2.clone.refs_2_) | copy-start | bytes 49156
  0.9 5.4 %copy-start = (f32[64]{0:T(128)S(1)}, f32[64]{0:T(128)}, u32[]{:S(2)}) copy-start(f32[64]{0:T(128)} %refs_0_.1) | copy-start | bytes 772
  0.9 11.0 %collective-permute-start = (bf16[256,128]{1,0:T(8,128)(2,1)S(1)}, bf16[256,128]{1,0:T(8,128)(2,1)S(1)}, u32[]{:S(2)}, u32[]{:S(2)}) collective-permute-start(bf16[256,128]{1,0:T(8,128)(2,1)S(1)} %slice.4), channel_id=1, source_target_pairs={{0,1},{1,2},{2,3},{3,4},{4,5},{5,6},{6,7},{7,8},{8,9},{9,10},{10,1... | collective-permute-start | bytes 196616 | tf_op jit(solution)/shard_map/ppermute | solution.py:22

commit v4 on v3

--- a/solution.py
+++ b/solution.py
@@ -67,16 +67,23 @@
     return total.astype(BF16)
 
 
-def filter_body(branches, antennas, count, proto, forget, pattern, x_hbm, out, weights, start, retain, x, sems):
+def filter_body(
+    branches, antennas, count, proto_hbm, forget, pattern, x_hbm,
+    out, weights, start, retain, x, proto, sems, proto_sem,
+):
     rows, frames = x_hbm.shape
+    small = pltpu.make_async_copy(proto_hbm, proto, proto_sem)
+    small.start()
     fetches = []
     for at in range(0, frames, STEP):
         there = (slice(None), slice(at, at + STEP))
         fetches.append(pltpu.make_async_copy(x_hbm.at[there], x.at[there], sems.at[at // STEP]))
         fetches[-1].start()
+    small.wait()
     tap_weights(proto, pattern, weights, branches, antennas)
+    for fetch in fetches:
+        fetch.wait()
     for at in range(0, frames, STEP):
-        fetches[at // STEP].wait()
         halo = x[:, at - HALO : at] if at else jnp.zeros((rows, HALO), BF16)
         longer = jnp.concatenate([halo, x[:, at : at + STEP]], axis=1)
         out[:, at : at + STEP] = filtered(weights, longer, STEP)
@@ -89,8 +96,9 @@
     taps = prototype.shape[0] // branches
     pattern = jnp.asarray(turn_pattern(branches, antennas))
     count = lax.axis_size("tm")
-    smem = pl.BlockSpec(memory_space=pltpu.SMEM)
+    hbm = pl.BlockSpec(memory_space=pltpu.HBM)
     vmem = pl.BlockSpec(memory_space=pltpu.VMEM)
+    stay = lambda value: pltpu.with_memory_space_constraint(value, pltpu.HBM)
     return pl.pallas_call(
         lambda *refs: filter_body(branches, antennas, count, *refs),
         out_shape=(
@@ -99,18 +107,20 @@
             jax.ShapeDtypeStruct((rows, HALO), BF16),
             jax.ShapeDtypeStruct((8, LANES), F32),
         ),
-        in_specs=[smem, smem, vmem, pl.BlockSpec(memory_space=pltpu.HBM)],
+        in_specs=[hbm, pl.BlockSpec(memory_space=pltpu.SMEM), vmem, hbm],
         out_specs=(vmem,) * 4,
         scratch_shapes=[
             pltpu.VMEM((rows, frames), BF16),
+            pltpu.SMEM(prototype.shape, F32),
             pltpu.SemaphoreType.DMA((frames // STEP,)),
+            pltpu.SemaphoreType.DMA,
         ],
         compiler_params=pltpu.CompilerParams(vmem_limit_bytes=GRANT),
         cost_estimate=pl.CostEstimate(
             flops=2 * taps * rows * rows * frames, bytes_accessed=4 * rows * frames, transcendentals=0
         ),
         name="filter_bank",
-    )(prototype, forget, pattern, pltpu.with_memory_space_constraint(flat, pltpu.HBM))
+    )(stay(prototype), forget, pattern, stay(flat))
 
 
 def head_body(tail, start, weights, alone, out):

time: 98.5 us -> 96.8 us (0.983)
  Pallas kernels: 13.6 us -> 12.1 us
    pallas_call x1, Pallas kernels: 5.59 us -> 4.09 us  [filter_bank(): pl.pallas_call(lambda *refs: filter_body(branches, antennas, count, *refs...]
  transfers between devices with their start and end apart: 1 -> 1, of which waited for: 0 -> 0; matrix products, arithmetic and copies ran while one was open for 0% -> 0% of each run, Pallas kernels for 6% -> 4%
where the time goes in v4:
time: 96.8 us; the launch traced here: 96.5 us
  blocking collectives  78.3 us (81%)
  Pallas kernels  12.1 us (12%)
  starting transfers between devices  4.57 us (5%)
    all_to_all x1, blocking collectives, per_device(): lax.all_to_all(spectra, 'chan', split_axis=0, concat_axis=0, tiled=True)  38.2 us
    all_to_all x1, blocking collectives, running_mean(): lax.all_to_all(pieces, 'tm', split_axis=0, concat_axis=0, tiled=True)  22.3 us
    all_to_all x1, blocking collectives, running_mean(): back = lax.all_to_all(mean, 'tm', split_axis=0, concat_axis=0, tiled=True)  17.8 us
    pallas_call x1, Pallas kernels, whiten(): pl.pallas_call(whiten_body, out_shape=jax.ShapeDtypeStruct(spectra.shape,...  6.59 us
    ppermute x1, starting transfers between devices, passed_along(): lax.ppermute(value, axis, [(source, source + 1) for source in range(count...  4.57 us
    pallas_call x1, Pallas kernels, filter_bank(): pl.pallas_call(lambda *refs: filter_body(branches, antennas, count, *refs...  4.09 us
  transfers between devices with their start and end apart: 1, of which 0 were waited for; matrix products, arithmetic and copies ran while one was open for 0% of the time, Pallas kernels for 4%

profile of v4, /device:TPU:1, one launch (start us, length us, event | category | flops | bytes accessed | tf_op | source)
XLA Modules:
  0.0 96.5 jit_solution(10608231046758212813)
XLA Ops:
  0.0 0.0 copy-start
  0.0 0.9 slice.4
  0.9 4.6 %collective-permute-start = (bf16[256,128]{1,0:T(8,128)(2,1)S(1)}, bf16[256,128]{1,0:T(8,128)(2,1)S(1)}, u32[]{:S(2)}, u32[]{:S(2)}) collective-permute-start(bf16[256,128]{1,0:T(8,128)(2,1)S(1)} %slice.4), channel_id=1, source_target_pairs={{0,1},{1,2},{2,3},{3,4},{4,5},{5,6},{6,7},{7,8},{8,9},{9,10},{10,1... | collective-permute-start | bytes 196616 | tf_op jit(solution)/shard_map/ppermute | solution.py:22
  6.1 0.0 copy-done
  6.1 4.1 %filter_bank.1 = (bf16[256,2048]{1,0:T(8,128)(2,1)S(1)}, bf16[256,2048]{1,0:T(8,128)(2,1)S(1)}, bf16[256,128]{1,0:T(8,128)(2,1)S(1)}, f32[8,128]{1,0:T(8,128)S(1)}) custom-call(f32[64]{0:T(128)} %refs_0_.1, f32[1]{0:T(128)S(6)} %copy.7.refs_1_, f32[16,256]{1,0:T(8,128)S(1)} %copy-done, bf16[256,2048]{1,0:T(8,128)(2,1)} %bitcast.12), custom_call_target="tpu_custom_call" | custom-call | flops 2147483648 | bytes 2097152 | tf_op jit(solution)/shard_map/filter_bank/pallas_call | solution.py:102
  10.2 0.0 collective-permute-done.tail
  10.2 0.6 with_history.1
  10.8 38.2 %all_to_all.15 = bf16[8,32,2048]{2,1,0:T(8,128)(2,1)S(1)} all-to-all(bf16[8,32,2048]{2,1,0:T(8,128)(2,1)S(1)} %bitcast.8), channel_id=1, replica_groups=mesh['chan'=8,'tm'=64] {'chan'}, dimensions={0} | all-to-all | bytes 2097152 | tf_op jit(solution)/shard_map/all_to_all | solution.py:315
  49.0 0.7 gram.1
  49.7 22.3 %all_to_all.16.refs_1_ = f32[64,8,128]{2,1,0:T(8,128)S(1)} all-to-all(f32[64,8,128]{2,1,0:T(8,128)S(1)} %bitcast.10), channel_id=1, replica_groups=mesh['chan'=8,'tm'=64] {'tm'}, dimensions={0} | all-to-all | bytes 524288 | tf_op jit(solution)/shard_map/all_to_all | solution.py:179
  72.0 0.1 running_mean.1
  72.1 17.8 %all_to_all.17 = f32[64,8,128]{2,1,0:T(8,128)S(1)} all-to-all(f32[64,8,128]{2,1,0:T(8,128)S(1)} %running_mean.1), channel_id=1, replica_groups=mesh['chan'=8,'tm'=64] {'tm'}, dimensions={0} | all-to-all | bytes 524288 | tf_op jit(solution)/shard_map/all_to_all | solution.py:188
  89.9 6.6 %whiten.1 = bf16[256,2048]{1,0:T(8,128)(2,1)} custom-call(f32[2,256,128]{2,1,0:T(8,128)S(1)} %bitcast.9, bf16[256,2048]{1,0:T(8,128)(2,1)S(1)} %bitcast.7), custom_call_target="tpu_custom_call" | custom-call | tf_op jit(solution)/shard_map/whiten/pallas_call | solution.py:293
Async XLA Ops:
  0.0 6.1 %copy-start = (f32[16,256]{1,0:T(8,128)S(1)}, f32[16,256]{1,0:T(8,128)}, u32[]{:S(2)}) copy-start(f32[16,256]{1,0:T(8,128)} %constant.2.clone.refs_2_) | copy-start | bytes 49156
  0.9 9.3 %collective-permute-start = (bf16[256,128]{1,0:T(8,128)(2,1)S(1)}, bf16[256,128]{1,0:T(8,128)(2,1)S(1)}, u32[]{:S(2)}, u32[]{:S(2)}) collective-permute-start(bf16[256,128]{1,0:T(8,128)(2,1)S(1)} %slice.4), channel_id=1, source_target_pairs={{0,1},{1,2},{2,3},{3,4},{4,5},{5,6},{6,7},{7,8},{8,9},{9,10},{10,1... | collective-permute-start | bytes 196616 | tf_op jit(solution)/shard_map/ppermute | solution.py:22

commit v5 on v4

--- a/solution.py
+++ b/solution.py
@@ -145,17 +145,24 @@
 
 
 def gram_body(x, out):
-    for part in range(out.shape[0]):
-        some = x[part * LANES : (part + 1) * LANES, :]
-        out[part] = lax.dot_general(x[...], some, (((1,), (1,)), ((), ())), preferred_element_type=F32)
-
-
-def gram(spectra):
-    side = spectra.shape[0]
+    dims = (((1,), (1,)), ((), ()))
+    low, high = x[:LANES, :], x[LANES:, :]
+    first = lax.dot_general(low, low, dims, preferred_element_type=F32)
+    second = lax.dot_general(high, high, dims, preferred_element_type=F32)
+    row = lax.broadcasted_iota(jnp.int32, (LANES, LANES), 0)
+    col = lax.broadcasted_iota(jnp.int32, (LANES, LANES), 1)
+    out[:LANES, :] = lax.dot_general(high, low, dims, preferred_element_type=F32)
+    out[LANES : 2 * LANES, :] = jnp.where(col <= row, first, second)
+    diagonal = jnp.sum(jnp.where(col == row, second, 0.0), axis=0, keepdims=True)
+    out[2 * LANES :, :] = jnp.broadcast_to(diagonal, (out.shape[0] - 2 * LANES, LANES))
+
+
+def gram(spectra, count):
+    rows = -(-(2 * LANES + 1) // count) * count
     vmem = pl.BlockSpec(memory_space=pltpu.VMEM)
     return pl.pallas_call(
         gram_body,
-        out_shape=jax.ShapeDtypeStruct((side // LANES, side, LANES), F32),
+        out_shape=jax.ShapeDtypeStruct((rows, LANES), F32),
         in_specs=[vmem],
         out_specs=vmem,
         compiler_params=pltpu.CompilerParams(vmem_limit_bytes=GRANT),
@@ -163,30 +170,36 @@
     )(spectra)
 
 
-def mean_body(frames, retained, pieces, out):
-    retain = retained[...]
-    moment = jnp.zeros((8, LANES), F32)
-    weight = jnp.zeros((8, LANES), F32)
-    for position in range(pieces.shape[0]):
-        moment = retain * moment + pieces[position]
+def mean_body(frames, count, retained, pieces, out):
+    each = pieces.shape[0] // count
+    retain = retained[:each, :]
+    moment = jnp.zeros((each, LANES), F32)
+    weight = jnp.zeros((each, LANES), F32)
+    for position in range(count):
+        here = slice(position * each, (position + 1) * each)
+        moment = retain * moment + pieces[here, :]
         weight = retain * weight + float(frames)
-        out[position] = moment / weight
+        out[here, :] = moment / weight
+
+
+def exchanged(packed):
+    count = lax.axis_size("tm")
+    pieces = packed.reshape(count, -1, 1, LANES)
+    return lax.all_to_all(pieces, "tm", split_axis=0, concat_axis=0, tiled=True).reshape(packed.shape)
 
 
 def running_mean(gram_now, retained, frames):
+    every = exchanged(gram_now)
     count = lax.axis_size("tm")
-    pieces = gram_now.reshape(count, -1, LANES)
-    every = lax.all_to_all(pieces, "tm", split_axis=0, concat_axis=0, tiled=True)
     mean = pl.pallas_call(
-        lambda *refs: mean_body(frames, *refs),
+        lambda *refs: mean_body(frames, count, *refs),
         out_shape=jax.ShapeDtypeStruct(every.shape, F32),
         in_specs=[pl.BlockSpec(memory_space=pltpu.VMEM)] * 2,
         out_specs=pl.BlockSpec(memory_space=pltpu.VMEM),
         compiler_params=pltpu.CompilerParams(vmem_limit_bytes=GRANT),
         name="running_mean",
     )(retained, every)
-    back = lax.all_to_all(mean, "tm", split_axis=0, concat_axis=0, tiled=True)
-    return back.reshape(gram_now.shape)
+    return exchanged(mean)
 
 
 def in_three(value):
@@ -199,8 +212,15 @@
 def whiten_body(cov, x, y_hbm, work, inverse, y, y_sem):
     side, frames = x.shape
     half = side // 2
-    work[:, :half] = cov[0]
-    work[:, half:] = cov[1]
+    packed = cov[half : 2 * half, :]
+    square_row = lax.broadcasted_iota(jnp.int32, (half, half), 0)
+    square_col = lax.broadcasted_iota(jnp.int32, (half, half), 1)
+    turned = packed.T
+    corner = jnp.where(square_col > square_row, packed, turned)
+    work[:half, :half] = jnp.where(square_col <= square_row, packed, turned)
+    work[half:, :half] = cov[:half, :]
+    work[:half, half:] = cov[:half, :].T
+    work[half:, half:] = jnp.where(square_col == square_row, cov[2 * half : 2 * half + 1, :], corner)
     stores = []
 
     def whitened(first, last):
@@ -314,7 +334,7 @@
     spectra = with_history(alone, weights, start, tail).reshape(branches, -1, frames)
     turned = lax.all_to_all(spectra, "chan", split_axis=0, concat_axis=0, tiled=True)
     turned = turned.reshape(-1, frames)
-    mean = running_mean(gram(turned), retained, frames)
+    mean = running_mean(gram(turned, lax.axis_size("tm")), retained, frames)
     return whiten(mean, turned)[None]
 
 

time: 96.8 us -> 93.4 us (0.965)
  blocking collectives: 78.3 us -> 74.8 us
    all_to_all x2, blocking collectives: 40.1 us -> 36.6 us  [exchanged(): lax.all_to_all(pieces, 'tm', split_axis=0, concat_axis=0, tiled=True)]
where the time goes in v5:
time: 93.4 us; the launch traced here: 93.1 us
  blocking collectives  74.8 us (80%)
  Pallas kernels  12.1 us (13%)
  starting transfers between devices  4.57 us (5%)
    all_to_all x1, blocking collectives, per_device(): lax.all_to_all(spectra, 'chan', split_axis=0, concat_axis=0, tiled=True)  38.2 us
    all_to_all x2, blocking collectives, exchanged(): lax.all_to_all(pieces, 'tm', split_axis=0, concat_axis=0, tiled=True)  36.6 us
    pallas_call x1, Pallas kernels, whiten(): pl.pallas_call(whiten_body, out_shape=jax.ShapeDtypeStruct(spectra.shape,...  6.72 us
    ppermute x1, starting transfers between devices, passed_along(): lax.ppermute(value, axis, [(source, source + 1) for source in range(count...  4.57 us
    pallas_call x1, Pallas kernels, filter_bank(): pl.pallas_call(lambda *refs: filter_body(branches, antennas, count, *refs...  4.09 us
  transfers between devices with their start and end apart: 1, of which 0 were waited for; matrix products, arithmetic and copies ran while one was open for 0% of the time, Pallas kernels for 4%

profile of v5, /device:TPU:1, one launch (start us, length us, event | category | flops | bytes accessed | tf_op | source)
XLA Modules:
  0.0 93.1 jit_solution(17048724675098168139)
XLA Ops:
  0.0 0.0 copy-start
  0.0 0.9 slice.4
  0.9 4.6 %collective-permute-start = (bf16[256,128]{1,0:T(8,128)(2,1)S(1)}, bf16[256,128]{1,0:T(8,128)(2,1)S(1)}, u32[]{:S(2)}, u32[]{:S(2)}) collective-permute-start(bf16[256,128]{1,0:T(8,128)(2,1)S(1)} %slice.4), channel_id=1, source_target_pairs={{0,1},{1,2},{2,3},{3,4},{4,5},{5,6},{6,7},{7,8},{8,9},{9,10},{10,1... | collective-permute-start | bytes 196616 | tf_op jit(solution)/shard_map/ppermute | solution.py:22
  6.1 0.0 copy-done
  6.1 4.1 %filter_bank.1 = (bf16[256,2048]{1,0:T(8,128)(2,1)S(1)}, bf16[256,2048]{1,0:T(8,128)(2,1)S(1)}, bf16[256,128]{1,0:T(8,128)(2,1)S(1)}, f32[8,128]{1,0:T(8,128)S(1)}) custom-call(f32[64]{0:T(128)} %refs_0_.1, f32[1]{0:T(128)S(6)} %copy.9.refs_1_, f32[16,256]{1,0:T(8,128)S(1)} %copy-done, bf16[256,2048]{1,0:T(8,128)(2,1)} %bitcast.16), custom_call_target="tpu_custom_call" | custom-call | flops 2147483648 | bytes 2097152 | tf_op jit(solution)/shard_map/filter_bank/pallas_call | solution.py:102
  10.2 0.0 collective-permute-done.tail
  10.2 0.6 with_history.1
  10.8 38.2 %all_to_all.15 = bf16[8,32,2048]{2,1,0:T(8,128)(2,1)S(1)} all-to-all(bf16[8,32,2048]{2,1,0:T(8,128)(2,1)S(1)} %bitcast.10), channel_id=1, replica_groups=mesh['chan'=8,'tm'=64] {'chan'}, dimensions={0} | all-to-all | bytes 2097152 | tf_op jit(solution)/shard_map/all_to_all | solution.py:335
  49.0 0.6 gram.1
  49.6 20.9 %all_to_all.16 = f32[64,5,1,128]{3,2,1,0:T(1,128)S(1)} all-to-all(f32[64,5,1,128]{3,2,1,0:T(1,128)S(1)} %bitcast.12), channel_id=1, replica_groups=mesh['chan'=8,'tm'=64] {'tm'}, dimensions={0} | all-to-all | bytes 327680 | tf_op jit(solution)/shard_map/all_to_all | solution.py:188
  70.5 0.1 running_mean.1
  70.6 15.7 %all_to_all.17 = f32[64,5,1,128]{3,2,1,0:T(1,128)S(1)} all-to-all(f32[64,5,1,128]{3,2,1,0:T(1,128)S(1)} %bitcast.14), channel_id=1, replica_groups=mesh['chan'=8,'tm'=64] {'tm'}, dimensions={0} | all-to-all | bytes 327680 | tf_op jit(solution)/shard_map/all_to_all | solution.py:188
  86.3 6.7 %whiten.1 = bf16[256,2048]{1,0:T(8,128)(2,1)} custom-call(f32[320,128]{1,0:T(8,128)S(1)} %bitcast.11, bf16[256,2048]{1,0:T(8,128)(2,1)S(1)} %bitcast.9), custom_call_target="tpu_custom_call" | custom-call | tf_op jit(solution)/shard_map/whiten/pallas_call | solution.py:313
Async XLA Ops:
  0.0 6.1 %copy-start = (f32[16,256]{1,0:T(8,128)S(1)}, f32[16,256]{1,0:T(8,128)}, u32[]{:S(2)}) copy-start(f32[16,256]{1,0:T(8,128)} %constant.2.clone.refs_2_) | copy-start | bytes 49156
  0.9 9.3 %collective-permute-start = (bf16[256,128]{1,0:T(8,128)(2,1)S(1)}, bf16[256,128]{1,0:T(8,128)(2,1)S(1)}, u32[]{:S(2)}, u32[]{:S(2)}) collective-permute-start(bf16[256,128]{1,0:T(8,128)(2,1)S(1)} %slice.4), channel_id=1, source_target_pairs={{0,1},{1,2},{2,3},{3,4},{4,5},{5,6},{6,7},{7,8},{8,9},{9,10},{10,1... | collective-permute-start | bytes 196616 | tf_op jit(solution)/shard_map/ppermute | solution.py:22

commit v6 on v5

--- a/solution.py
+++ b/solution.py
@@ -81,12 +81,15 @@
         fetches[-1].start()
     small.wait()
     tap_weights(proto, pattern, weights, branches, antennas)
-    for fetch in fetches:
+    for fetch in fetches[:2]:
         fetch.wait()
     for at in range(0, frames, STEP):
-        halo = x[:, at - HALO : at] if at else jnp.zeros((rows, HALO), BF16)
-        longer = jnp.concatenate([halo, x[:, at : at + STEP]], axis=1)
-        out[:, at : at + STEP] = filtered(weights, longer, STEP)
+        if at == 2 * STEP:
+            for fetch in fetches[2:]:
+                fetch.wait()
+        first = max(at, HALO)
+        longer = x[:, first - HALO : at + STEP]
+        out[:, first : at + STEP] = filtered(weights, longer, at + STEP - first)
     start[...] = x[:, :HALO]
     retain[...] = jnp.exp(jnp.full(retain.shape, -forget[0] / count, F32))
 

time: 93.4 us -> 93.4 us (level)
  no operation moved by 1% of the time
where the time goes in v6:
time: 93.4 us; the launch traced here: 93.1 us
  blocking collectives  74.8 us (80%)
  Pallas kernels  12.1 us (13%)
  starting transfers between devices  4.57 us (5%)
    all_to_all x1, blocking collectives, per_device(): lax.all_to_all(spectra, 'chan', split_axis=0, concat_axis=0, tiled=True)  38.2 us
    all_to_all x2, blocking collectives, exchanged(): lax.all_to_all(pieces, 'tm', split_axis=0, concat_axis=0, tiled=True)  36.6 us
    pallas_call x1, Pallas kernels, whiten(): pl.pallas_call(whiten_body, out_shape=jax.ShapeDtypeStruct(spectra.shape,...  6.72 us
    ppermute x1, starting transfers between devices, passed_along(): lax.ppermute(value, axis, [(source, source + 1) for source in range(count...  4.57 us
    pallas_call x1, Pallas kernels, filter_bank(): pl.pallas_call(lambda *refs: filter_body(branches, antennas, count, *refs...  4.11 us
  transfers between devices with their start and end apart: 1, of which 0 were waited for; matrix products, arithmetic and copies ran while one was open for 0% of the time, Pallas kernels for 4%

profile of v6, /device:TPU:1, one launch (start us, length us, event | category | flops | bytes accessed | tf_op | source)
XLA Modules:
  0.0 93.1 jit_solution(1161385988233432396)
XLA Ops:
  0.0 0.0 copy-start
  0.0 0.9 slice.4
  0.9 4.6 %collective-permute-start = (bf16[256,128]{1,0:T(8,128)(2,1)S(1)}, bf16[256,128]{1,0:T(8,128)(2,1)S(1)}, u32[]{:S(2)}, u32[]{:S(2)}) collective-permute-start(bf16[256,128]{1,0:T(8,128)(2,1)S(1)} %slice.4), channel_id=1, source_target_pairs={{0,1},{1,2},{2,3},{3,4},{4,5},{5,6},{6,7},{7,8},{8,9},{9,10},{10,1... | collective-permute-start | bytes 196616 | tf_op jit(solution)/shard_map/ppermute | solution.py:22
  6.1 0.0 copy-done
  6.1 4.1 %filter_bank.1 = (bf16[256,2048]{1,0:T(8,128)(2,1)S(1)}, bf16[256,2048]{1,0:T(8,128)(2,1)S(1)}, bf16[256,128]{1,0:T(8,128)(2,1)S(1)}, f32[8,128]{1,0:T(8,128)S(1)}) custom-call(f32[64]{0:T(128)} %refs_0_.1, f32[1]{0:T(128)S(6)} %copy.9.refs_1_, f32[16,256]{1,0:T(8,128)S(1)} %copy-done, bf16[256,2048]{1,0:T(8,128)(2,1)} %bitcast.16), custom_call_target="tpu_custom_call" | custom-call | flops 2147483648 | bytes 2097152 | tf_op jit(solution)/shard_map/filter_bank/pallas_call | solution.py:105
  10.2 0.0 collective-permute-done.tail
  10.2 0.6 with_history.1
  10.8 38.2 %all_to_all.15 = bf16[8,32,2048]{2,1,0:T(8,128)(2,1)S(1)} all-to-all(bf16[8,32,2048]{2,1,0:T(8,128)(2,1)S(1)} %bitcast.10), channel_id=1, replica_groups=mesh['chan'=8,'tm'=64] {'chan'}, dimensions={0} | all-to-all | bytes 2097152 | tf_op jit(solution)/shard_map/all_to_all | solution.py:338
  49.1 0.6 gram.1
  49.6 20.9 %all_to_all.16 = f32[64,5,1,128]{3,2,1,0:T(1,128)S(1)} all-to-all(f32[64,5,1,128]{3,2,1,0:T(1,128)S(1)} %bitcast.12), channel_id=1, replica_groups=mesh['chan'=8,'tm'=64] {'tm'}, dimensions={0} | all-to-all | bytes 327680 | tf_op jit(solution)/shard_map/all_to_all | solution.py:191
  70.5 0.1 running_mean.1
  70.7 15.7 %all_to_all.17 = f32[64,5,1,128]{3,2,1,0:T(1,128)S(1)} all-to-all(f32[64,5,1,128]{3,2,1,0:T(1,128)S(1)} %bitcast.14), channel_id=1, replica_groups=mesh['chan'=8,'tm'=64] {'tm'}, dimensions={0} | all-to-all | bytes 327680 | tf_op jit(solution)/shard_map/all_to_all | solution.py:191
  86.4 6.7 %whiten.1 = bf16[256,2048]{1,0:T(8,128)(2,1)} custom-call(f32[320,128]{1,0:T(8,128)S(1)} %bitcast.11, bf16[256,2048]{1,0:T(8,128)(2,1)S(1)} %bitcast.9), custom_call_target="tpu_custom_call" | custom-call | tf_op jit(solution)/shard_map/whiten/pallas_call | solution.py:316
Async XLA Ops:
  0.0 6.1 %copy-start = (f32[16,256]{1,0:T(8,128)S(1)}, f32[16,256]{1,0:T(8,128)}, u32[]{:S(2)}) copy-start(f32[16,256]{1,0:T(8,128)} %constant.2.clone.refs_2_) | copy-start | bytes 49156
  0.9 9.4 %collective-permute-start = (bf16[256,128]{1,0:T(8,128)(2,1)S(1)}, bf16[256,128]{1,0:T(8,128)(2,1)S(1)}, u32[]{:S(2)}, u32[]{:S(2)}) collective-permute-start(bf16[256,128]{1,0:T(8,128)(2,1)S(1)} %slice.4), channel_id=1, source_target_pairs={{0,1},{1,2},{2,3},{3,4},{4,5},{5,6},{6,7},{7,8},{8,9},{9,10},{10,1... | collective-permute-start | bytes 196616 | tf_op jit(solution)/shard_map/ppermute | solution.py:22
